TPU v7x, 128 devices: a whole 4x4x4 slice. The times are simulated.
128 devices in a mesh: dp: 8 (over z, core), vocab: 16 (over y, x).
Axes of the slice: x: 4, y: 4, z: 4, core: 2. Of those that a mesh axis runs over, the one named last changes fastest.
Arguments:
- hidden: bfloat16 [12288, 896], P(('dp', 'vocab')), may hold values from -400 to 400
- target_ids: int32 [12288], P('dp'), may hold values from 0 to 151935
- owner: int32 [8, 48], P('dp'), may hold values from 0 to 47, each once within a row
- head: bfloat16 [896, 151936], P(None, 'vocab'), may hold values from -0.1875 to 0.1875
Outputs:
- owned_loss: float32 [384, 32], P(('dp', 'vocab'))
Inputs may be any that keep to these rules, and one draw needn't show every extreme that they name: Each row of owner names every slot once.
All inputs are finite; a program needn't handle non-finite values.
Results may differ from a plain program's by a relative error of at most 0.0003.
Values may be sent and summed in bfloat16 or wider, within the bound.
A program may use at most 128 MiB of HBM per device.

v0:
```python
import math
import jax
import jax.numpy as jnp
from jax import lax
from jax.sharding import PartitionSpec as P


def side_by_side(arrays, axis, split_dim, concat_dim, along):
    ends, at = ([], 0)
    for a in arrays[:-1]:
        at += a.shape[along]
        ends.append(at)
    both = jnp.concatenate(arrays, axis=along)
    return tuple(
        jnp.split(
            lax.all_to_all(both, axis, split_axis=split_dim, concat_axis=concat_dim, tiled=True),
            ends,
            axis=along,
        )
    )


def local(hidden, target_ids, owner, head):
    width = head.shape[1]
    base = lax.axis_index("vocab") * width

    def partials(rows, labels):
        logits = jnp.dot(rows, head, preferred_element_type=jnp.float32)
        peak = jnp.max(logits, axis=1)
        expsum = jnp.sum(jnp.exp(logits - peak[:, None]), axis=1)
        column = lax.broadcasted_iota(jnp.int32, logits.shape, 1)
        picked = jnp.sum(jnp.where(column == (labels - base)[:, None], logits, 0.0), axis=1)
        return jnp.stack((peak, expsum, picked), 0)

    gathered = lax.all_gather(hidden, "vocab", axis=0, tiled=True)
    count = gathered.shape[0]
    step_rows = math.gcd(count, 512)
    split_rows = gathered.reshape(count // step_rows, step_rows, gathered.shape[1])
    split_labels = target_ids.reshape(count // step_rows, step_rows)
    results = lax.map(lambda pair: partials(pair[0], pair[1]), (split_rows, split_labels))
    stats = jnp.transpose(results, (1, 0, 2)).reshape(3, count)
    peak, expsum, picked = (stats[0], stats[1], stats[2])
    seq_group = owner.shape[1]
    length = target_ids.shape[0] // seq_group
    shards = lax.axis_size("vocab")
    own_count = seq_group // shards
    slots_row = owner[0]
    slot_index = lax.broadcasted_iota(jnp.int32, (seq_group, seq_group), 0)
    reorder = (slot_index == slots_row[None, :]).astype(jnp.float32)
    ordered_peak = jnp.dot(
        reorder, peak.reshape(seq_group, length), precision=lax.Precision.HIGHEST
    )
    ordered_sum = jnp.dot(
        reorder, expsum.reshape(seq_group, length), precision=lax.Precision.HIGHEST
    )
    ordered_pick = jnp.dot(
        reorder, picked.reshape(seq_group, length), precision=lax.Precision.HIGHEST
    )
    got_peak, got_sum, got_pick = side_by_side(
        (ordered_peak, ordered_sum, ordered_pick), "vocab", 0, 0, 1
    )
    got_peak = got_peak.reshape(shards, own_count, length)
    got_sum = got_sum.reshape(shards, own_count, length)
    got_pick = got_pick.reshape(shards, own_count, length)
    top = jnp.max(got_peak, axis=0)
    total = jnp.sum(got_sum * jnp.exp(got_peak - top[None]), axis=0)
    return top + jnp.log(total) - jnp.sum(got_pick, axis=0)


def solution(mesh):
    return jax.shard_map(
        local,
        mesh=mesh,
        in_specs=(P(("dp", "vocab"), None), P("dp"), P("dp", None), P(None, "vocab")),
        out_specs=P(("dp", "vocab"), None),
        check_vma=False,
    )
```

profile of v0, /device:TPU:0, one launch (start us, length us, event | category | flops | bytes accessed | tf_op | source)
XLA Modules:
  0.0 162.2 jit_solution(14684987293334065380)
XLA Ops:
  6.5 0.0 all-gather.2.cloned.1.call-start
  6.5 0.7 all-gather.2.cloned.1.call-update
  7.3 0.7 reshape.34
  8.0 50.4 %all-gather.2.cloned.1.call-done = bf16[1536,896]{1,0:T(8,128)(2,1)} async-done(((bf16[96,896]{1,0:T(8,128)(2,1)}), bf16[1536,896]{1,0:T(8,128)(2,1)}) %all-gather.2.cloned.1.call-update) | async-done | bytes 2752528 | tf_op jit(solution)/shard_map/all_gather | solution.py:35
  58.3 0.0 copy-start
  58.3 83.0 %while.10 = (s32[]{:T(128)}, f32[3,3,512]{2,1,0:T(4,128)S(1)}, bf16[3,512,896]{2,1,0:T(8,128)(2,1)}, bf16[896,9496]{0,1:T(8,128)(2,1)}, s32[3,512]{1,0:T(4,128)S(1)}, /*index=5*/s32[]{:T(128)}, s32[]{:T(128)}) while((s32[]{:T(128)}, f32[3,3,512]{2,1,0:T(4,128)S(1)}, bf16[3,512,896]{2,1,0:T(8,128)(2,1)}, bf16[896,9496]{0,1:T(8,128)(2,1)}, ...), condition=%wide.region_4.5_spmd, body=%wide.region_0.4_spmd.sunk | while | flops 8741791744 | bytes 56859224 | solution.py:40
  58.3 17.9 %fusion.21 = (f32[512]{0:T(512)S(1)}, f32[512,9496]{0,1:T(8,128)}) fusion(bf16[896,9496]{0,1:T(8,128)(2,1)} %get-tuple-element.122, bf16[3,512,896]{2,1,0:T(8,128)(2,1)} %get-tuple-element.121, s32[]{:T(128)} %get-tuple-element.112), kind=kOutput, calls=%fused_computation.23.clone.1 | convolution fusion | flops 8717479936 | bytes 37384704 | tf_op jit(solution)/shard_map/while/body/eval_jaxpr/dot_general | solution.py:28
  76.3 9.6 %exponential_reduce_fusion.2 = (f32[512]{0:T(512)S(1)}, f32[512]{0:T(512)S(1)}) fusion(f32[512,9496]{0,1:T(8,128)} %get-tuple-element.101, f32[512]{0:T(512)S(1)} %get-tuple-element.102, s32[512]{0:T(512)S(1)} %bitcast.34), kind=kLoop, calls=%fused_computation.2.clone.1 | loop fusion | flops 24308736 | bytes 19456000 | tf_op jit(solution)/shard_map/while/body/eval_jaxpr/reduce_sum | solution.py:30
  86.0 18.0 %fusion.21 = (f32[512]{0:T(512)S(1)}, f32[512,9496]{0,1:T(8,128)}) fusion(bf16[896,9496]{0,1:T(8,128)(2,1)} %get-tuple-element.122, bf16[3,512,896]{2,1,0:T(8,128)(2,1)} %get-tuple-element.121, s32[]{:T(128)} %get-tuple-element.112), kind=kOutput, calls=%fused_computation.23.clone.1 | convolution fusion | flops 8717479936 | bytes 37384704 | tf_op jit(solution)/shard_map/while/body/eval_jaxpr/dot_general | solution.py:28
  104.0 9.6 %exponential_reduce_fusion.2 = (f32[512]{0:T(512)S(1)}, f32[512]{0:T(512)S(1)}) fusion(f32[512,9496]{0,1:T(8,128)} %get-tuple-element.101, f32[512]{0:T(512)S(1)} %get-tuple-element.102, s32[512]{0:T(512)S(1)} %bitcast.34), kind=kLoop, calls=%fused_computation.2.clone.1 | loop fusion | flops 24308736 | bytes 19456000 | tf_op jit(solution)/shard_map/while/body/eval_jaxpr/reduce_sum | solution.py:30
  113.7 17.9 %fusion.21 = (f32[512]{0:T(512)S(1)}, f32[512,9496]{0,1:T(8,128)}) fusion(bf16[896,9496]{0,1:T(8,128)(2,1)} %get-tuple-element.122, bf16[3,512,896]{2,1,0:T(8,128)(2,1)} %get-tuple-element.121, s32[]{:T(128)} %get-tuple-element.112), kind=kOutput, calls=%fused_computation.23.clone.1 | convolution fusion | flops 8717479936 | bytes 37384704 | tf_op jit(solution)/shard_map/while/body/eval_jaxpr/dot_general | solution.py:28
  131.6 9.6 %exponential_reduce_fusion.2 = (f32[512]{0:T(512)S(1)}, f32[512]{0:T(512)S(1)}) fusion(f32[512,9496]{0,1:T(8,128)} %get-tuple-element.101, f32[512]{0:T(512)S(1)} %get-tuple-element.102, s32[512]{0:T(512)S(1)} %bitcast.34), kind=kLoop, calls=%fused_computation.2.clone.1 | loop fusion | flops 24308736 | bytes 19456000 | tf_op jit(solution)/shard_map/while/body/eval_jaxpr/reduce_sum | solution.py:30
  141.3 0.1 slice_reduce_fusion.2
  141.4 0.1 reshape_squeeze.11
  141.5 0.1 reshape_squeeze.10
  141.5 0.0 copy-done
  141.5 0.2 fusion.5
  141.7 0.2 fusion.6
  141.9 0.1 reshape_squeeze.9
  142.0 0.2 fusion.7
  142.3 0.1 copy.6
  142.4 12.1 %all_to_all.12 = f32[16,3,96]{2,1,0:T(4,128)S(1)} all-to-all(f32[16,3,96]{2,1,0:T(4,128)S(1)} %all_to_all.8), channel_id=1, replica_groups=mesh['dp'=8,'vocab'=16] {'vocab'}, dimensions={0} | all-to-all | bytes 36864 | tf_op jit(solution)/shard_map/all_to_all | solution.py:16
  154.5 0.1 fusion.12
  154.7 0.6 add_subtract_fusion
  (16 shorter events, 0.3 us)
Async XLA Ops:
  6.5 51.8 %all-gather.2.cloned.1.call-start = ((), (), s32[]{:S(2)}) async-start(), calls=%async_computation.1 | async-start | bytes 2924544 | tf_op jit(solution)/shard_map/all_gather | solution.py:35
  58.3 83.2 %copy-start = (s32[1,48]{1,0:T(1,128)S(1)}, s32[1,48]{1,0:T(1,128)}, u32[]{:S(2)}) copy-start(s32[1,48]{1,0:T(1,128)} %param.8) | copy-start | bytes 580
Sparse Core Ops, SparseCore 0:
  9.5 48.8 all-gather.1
where the time goes:
time: 163 us; the launch traced here: 162 us
  matrix products  54.5 us (33%)
  waiting for transfers between devices  51.1 us (31%)
  other arithmetic  29.7 us (18%)
  between operations  13.5 us (8%)
  blocking collectives  12.1 us (7%)
    dot_general x3, matrix products, partials(): logits = jnp.dot(rows, head, preferred_element_type=jnp.float32)  53.9 us
    all_gather x1, waiting for transfers between devices, local(): gathered = lax.all_gather(hidden, 'vocab', axis=0, tiled=True)  50.4 us
    reduce_sum x3, other arithmetic, partials(): expsum = jnp.sum(jnp.exp(logits - peak[:, None]), axis=1)  28.9 us
    all_to_all x1, blocking collectives, side_by_side(): lax.all_to_all(both, axis, split_axis=split_dim, concat_axis=concat_dim,...  12.1 us
  transfers between devices with their start and end apart: 1, of which 1 were waited for; matrix products, arithmetic and copies ran while one was open for 0% of the time, Pallas kernels for 0%

commit v1 on v0

--- a/solution.py
+++ b/solution.py
@@ -32,7 +32,8 @@
         picked = jnp.sum(jnp.where(column == (labels - base)[:, None], logits, 0.0), axis=1)
         return jnp.stack((peak, expsum, picked), 0)
 
-    gathered = lax.all_gather(hidden, "vocab", axis=0, tiled=True)
+    sent = jnp.stack([hidden] * lax.axis_size("vocab"))
+    gathered = jnp.concatenate(lax.all_to_all(sent, "vocab", 0, 0), axis=0)
     count = gathered.shape[0]
     step_rows = math.gcd(count, 512)
     split_rows = gathered.reshape(count // step_rows, step_rows, gathered.shape[1])

time: 163 us -> 147 us (0.902)
  between operations: 13.5 us -> 0.07 us
  waiting for transfers between devices: 51.1 us -> 41 us
  starting transfers between devices: 0.01 us -> 7.15 us
  local copies, waits for them, and re-layouts: 1.24 us -> 3.92 us
    all_gather x1 -> x0, waiting for transfers between devices: 50.4 us -> none  [local(): gathered = lax.all_gather(hidden, 'vocab', axis=0, tiled=True)]
    all_to_all x0 -> x1, waiting for transfers between devices: none -> 41 us  [local(): gathered = jnp.concatenate(lax.all_to_all(sent, 'vocab', 0, 0), axis=0)]
    all_to_all x0 -> x1, starting transfers between devices: none -> 7.15 us  [local(): gathered = jnp.concatenate(lax.all_to_all(sent, 'vocab', 0, 0), axis=0)]
    another operation x0 -> x1, local copies, waits for them, and re-layouts: none -> 2.68 us  [local(): sent = jnp.stack([hidden] * lax.axis_size('vocab'))]
where the time goes in v1:
time: 147 us
  matrix products  53.7 us (37%)
  waiting for transfers between devices  41 us (28%)
  other arithmetic  29.7 us (20%)
  blocking collectives  11.3 us (8%)
  starting transfers between devices  7.15 us (5%)
  local copies, waits for them, and re-layouts  3.92 us (3%)
    dot_general x3, matrix products, partials(): logits = jnp.dot(rows, head, preferred_element_type=jnp.float32)  53.1 us
    all_to_all x1, waiting for transfers between devices, local(): gathered = jnp.concatenate(lax.all_to_all(sent, 'vocab', 0, 0), axis=0)  41 us
    reduce_sum x3, other arithmetic, partials(): expsum = jnp.sum(jnp.exp(logits - peak[:, None]), axis=1)  28.9 us
    all_to_all x1, blocking collectives, side_by_side(): lax.all_to_all(both, axis, split_axis=split_dim, concat_axis=concat_dim,...  11.3 us
    all_to_all x1, starting transfers between devices, local(): gathered = jnp.concatenate(lax.all_to_all(sent, 'vocab', 0, 0), axis=0)  7.15 us
  transfers between devices with their start and end apart: 1, of which 1 were waited for; matrix products, arithmetic and copies ran while one was open for 0% of the time, Pallas kernels for 0%

profile of v1, /device:TPU:0, one launch (start us, length us, event | category | flops | bytes accessed | tf_op | source)
XLA Modules:
  0.0 146.9 jit_solution(6855226768886785421)
XLA Ops:
  0.0 2.7 %stack.10 = bf16[16,96,896]{2,1,0:T(8,128)(2,1)} broadcast(bf16[96,896]{1,0:T(8,128)(2,1)} %param.6), dimensions={1,2} | broadcast | bytes 2924544 | tf_op jit(solution)/shard_map/stack | solution.py:35
  2.7 7.1 %all-to-all-start = ((bf16[16,96,896]{2,1,0:T(8,128)(2,1)}), bf16[16,96,896]{2,1,0:T(8,128)(2,1)S(1)}, u32[]{:S(2)}, u32[]{:S(2)}) async-start(bf16[16,96,896]{2,1,0:T(8,128)(2,1)} %stack.10), calls=%async_computation | async-start | bytes 5505024 | tf_op jit(solution)/shard_map/all_to_all | solution.py:36
  9.8 0.7 reshape.32
  10.6 41.0 %all-to-all-done = bf16[16,96,896]{2,1,0:T(8,128)(2,1)S(1)} async-done(((bf16[16,96,896]{2,1,0:T(8,128)(2,1)}), bf16[16,96,896]{2,1,0:T(8,128)(2,1)S(1)}, u32[]{:S(2)}, u32[]{:S(2)}) %all-to-all-start) | async-done | bytes 2752544 | tf_op jit(solution)/shard_map/all_to_all | solution.py:36
  51.6 0.0 copy-start
  51.6 82.1 %while.10 = (s32[]{:T(128)}, f32[3,3,512]{2,1,0:T(4,128)S(1)}, bf16[3,512,896]{2,1,0:T(8,128)(2,1)S(1)}, bf16[896,9496]{0,1:T(8,128)(2,1)}, s32[3,512]{1,0:T(4,128)S(1)}, /*index=5*/s32[]{:T(128)}, s32[]{:T(128)}) while((s32[]{:T(128)}, f32[3,3,512]{2,1,0:T(4,128)S(1)}, bf16[3,512,896]{2,1,0:T(8,128)(2,1)S(1)}, bf16[896,9496]{0,1:T(8,128)(2,1)}, ...), condition=%wide.region_4.5_spmd, body=%wide.region_0.4_spmd.sunk | while | flops 8741791744 | bytes 56858716 | solution.py:41
  51.6 17.7 %fusion.21 = (f32[512]{0:T(512)S(1)}, f32[512,9496]{0,1:T(8,128)}) fusion(bf16[896,9496]{0,1:T(8,128)(2,1)} %get-tuple-element.122, bf16[3,512,896]{2,1,0:T(8,128)(2,1)S(1)} %get-tuple-element.121, s32[]{:T(128)} %get-tuple-element.112), kind=kOutput, calls=%fused_computation.23.clone.1 | convolution fusion | flops 8717479936 | bytes 37384196 | tf_op jit(solution)/shard_map/while/body/eval_jaxpr/dot_general | solution.py:28
  69.3 9.6 %exponential_reduce_fusion.2 = (f32[512]{0:T(512)S(1)}, f32[512]{0:T(512)S(1)}) fusion(f32[512,9496]{0,1:T(8,128)} %get-tuple-element.101, f32[512]{0:T(512)S(1)} %get-tuple-element.102, s32[512]{0:T(512)S(1)} %bitcast.35), kind=kLoop, calls=%fused_computation.2.clone.1 | loop fusion | flops 24308736 | bytes 19456000 | tf_op jit(solution)/shard_map/while/body/eval_jaxpr/reduce_sum | solution.py:30
  79.0 17.7 %fusion.21 = (f32[512]{0:T(512)S(1)}, f32[512,9496]{0,1:T(8,128)}) fusion(bf16[896,9496]{0,1:T(8,128)(2,1)} %get-tuple-element.122, bf16[3,512,896]{2,1,0:T(8,128)(2,1)S(1)} %get-tuple-element.121, s32[]{:T(128)} %get-tuple-element.112), kind=kOutput, calls=%fused_computation.23.clone.1 | convolution fusion | flops 8717479936 | bytes 37384196 | tf_op jit(solution)/shard_map/while/body/eval_jaxpr/dot_general | solution.py:28
  96.7 9.6 %exponential_reduce_fusion.2 = (f32[512]{0:T(512)S(1)}, f32[512]{0:T(512)S(1)}) fusion(f32[512,9496]{0,1:T(8,128)} %get-tuple-element.101, f32[512]{0:T(512)S(1)} %get-tuple-element.102, s32[512]{0:T(512)S(1)} %bitcast.35), kind=kLoop, calls=%fused_computation.2.clone.1 | loop fusion | flops 24308736 | bytes 19456000 | tf_op jit(solution)/shard_map/while/body/eval_jaxpr/reduce_sum | solution.py:30
  106.4 17.7 %fusion.21 = (f32[512]{0:T(512)S(1)}, f32[512,9496]{0,1:T(8,128)}) fusion(bf16[896,9496]{0,1:T(8,128)(2,1)} %get-tuple-element.122, bf16[3,512,896]{2,1,0:T(8,128)(2,1)S(1)} %get-tuple-element.121, s32[]{:T(128)} %get-tuple-element.112), kind=kOutput, calls=%fused_computation.23.clone.1 | convolution fusion | flops 8717479936 | bytes 37384196 | tf_op jit(solution)/shard_map/while/body/eval_jaxpr/dot_general | solution.py:28
  124.1 9.6 %exponential_reduce_fusion.2 = (f32[512]{0:T(512)S(1)}, f32[512]{0:T(512)S(1)}) fusion(f32[512,9496]{0,1:T(8,128)} %get-tuple-element.101, f32[512]{0:T(512)S(1)} %get-tuple-element.102, s32[512]{0:T(512)S(1)} %bitcast.35), kind=kLoop, calls=%fused_computation.2.clone.1 | loop fusion | flops 24308736 | bytes 19456000 | tf_op jit(solution)/shard_map/while/body/eval_jaxpr/reduce_sum | solution.py:30
  133.7 0.1 slice_reduce_fusion.2
  133.8 0.1 reshape_squeeze.11
  133.9 0.1 reshape_squeeze.10
  133.9 0.0 copy-done
  133.9 0.2 fusion.5
  134.1 0.2 fusion.6
  134.3 0.1 reshape_squeeze.9
  134.4 0.2 fusion.7
  134.7 0.1 copy.6
  134.8 11.3 %all_to_all.17 = f32[16,3,96]{2,1,0:T(4,128)S(1)} all-to-all(f32[16,3,96]{2,1,0:T(4,128)S(1)} %all_to_all.12), channel_id=1, replica_groups=mesh['dp'=8,'vocab'=16] {'vocab'}, dimensions={0} | all-to-all | bytes 36864 | tf_op jit(solution)/shard_map/all_to_all | solution.py:16
  146.0 0.1 fusion.12
  146.3 0.6 add_subtract_fusion
  (16 shorter events, 0.3 us)
Async XLA Ops:
  2.7 48.9 %all-to-all-start = ((bf16[16,96,896]{2,1,0:T(8,128)(2,1)}), bf16[16,96,896]{2,1,0:T(8,128)(2,1)S(1)}, u32[]{:S(2)}, u32[]{:S(2)}) async-start(bf16[16,96,896]{2,1,0:T(8,128)(2,1)} %stack.10), calls=%async_computation | async-start | bytes 5505024 | tf_op jit(solution)/shard_map/all_to_all | solution.py:36
  51.6 82.4 %copy-start = (s32[1,48]{1,0:T(1,128)S(1)}, s32[1,48]{1,0:T(1,128)}, u32[]{:S(2)}) copy-start(s32[1,48]{1,0:T(1,128)} %param.8) | copy-start | bytes 580
